TPU v7x, 32 devices: a whole 2x2x4 slice. The times are simulated.
32 devices in a mesh: dp: 8 (over z, x), shard: 4 (over y, core).
Axes of the slice: x: 2, y: 2, z: 4, core: 2. Of those that a mesh axis runs over, the one named last changes fastest.
Arguments:
- noisy: float32 [128, 256, 16], P(('dp', 'shard')), may hold values from -6 to 6
- velocity: float32 [128, 256, 16], P(('dp', 'shard')), may hold values from -6 to 6
- tstep_idx: int32 [128], P(('dp', 'shard')), may hold values from 0 to 999
- class_ids: int32 [128], P(('dp', 'shard')), may hold values from 0 to 1000
- time_weight: float32 [128], P(('dp', 'shard')), may hold values from 0.3 to 3
- dino: bfloat16 [128, 256, 768], P(('dp', 'shard')), may hold values from -6 to 6
- owner_map: int32 [12], replicated, may hold values from 0 to 11, each once
- adam_flat: float32 [2129920], P(('dp', 'shard')), may hold values from -4 to 4
- adam_m: float32 [2129920], P(('dp', 'shard')), may hold values from -0.015625 to 0.015625
- adam_v: float32 [2129920], P(('dp', 'shard')), may hold values from 1e-06 to 0.0001
- blocks_w: float32 [12, 384, 384], P('shard'), may hold values from -0.3125 to 0.3125
- stat_left: float32 [12, 384, 384], P('shard'), may hold values from -0.005 to 0.01, as said below
- stat_right: float32 [12, 384, 384], P('shard'), may hold values from -0.005 to 0.01, as said below
- root_left: float32 [12, 384, 384], P('shard'), may hold values from -3 to 3, as said below
- root_right: float32 [12, 384, 384], P('shard'), may hold values from -3 to 3, as said below
Outputs:
- loss: float32 [], replicated
- block_update: float32 [12, 384, 384], P('shard')
- stat_left_new: float32 [12, 384, 384], P('shard')
- stat_right_new: float32 [12, 384, 384], P('shard')
- adam_update: float32 [2129920], P(('dp', 'shard'))
- adam_m_new: float32 [2129920], P(('dp', 'shard'))
- adam_v_new: float32 [2129920], P(('dp', 'shard'))
Inputs may be any that keep to these rules, and one draw needn't show every extreme that they name: `owner_map`: each block number appears once. `stat_left`: each slot is symmetric positive definite. `stat_right`: each slot is symmetric positive definite. `root_left`: each slot is symmetric positive definite. `root_right`: each slot is symmetric positive definite.
All inputs are finite; a program needn't handle non-finite values.
Results may differ from a plain program's by a relative error of at most 0.0097.
Values may be sent and summed in bfloat16 or wider, within the bound.
No kernel may reach another device: no remote copies, remote signals or barrier semaphores. Data moves between devices by JAX's collectives and lax.ppermute only.
A program may use at most 192 MiB of HBM per device.

v0:
```python
import functools
import math
import jax
import jax.numpy as jnp
from jax import lax
from jax.sharding import PartitionSpec as P

D = 384
HEADS = 6
HDIM = 64
F = 1536
PD = 16
GRID = 16
SEQ = 256
FREQ = 256
NCLS = 1001
DINO = 768
STEP = 10
NBLK = 12
ADAM_LEN = 2125072
ADAM_PAD = 2129920
HIGHEST = lax.Precision.HIGHEST
BETA_ONE = 0.9
BETA_TWO = 0.95
ADAM_EPS = 1e-08
ADAM_RATE = 0.01
DECAY_RATE = 0.1
STAT_BETA = 0.9
SHAMPOO_RATE = 0.02
RMS_EPS = 1e-08
REPA_WEIGHT = 0.5
NORM_EPS = 1e-06


def segment_shapes():
    return [
        (PD, D),
        (D,),
        (FREQ, D),
        (D,),
        (D, D),
        (D,),
        (NCLS, D),
        (D, 6 * D),
        (6 * D,),
        (D,),
        (D,),
        (D,),
        (F,),
        (D,),
        (D, 2 * D),
        (2 * D,),
        (D, PD),
        (PD,),
        (D, DINO),
        (DINO,),
    ]


def unflatten(flat):
    pieces = []
    offset = 0
    for seg_dims in segment_shapes():
        length = math.prod(seg_dims)
        pieces.append(flat[offset : offset + length].reshape(seg_dims))
        offset += length
    return pieces


def position_table():
    quarter = D // 4
    frequencies = 1.0 / 10000.0 ** (jnp.arange(quarter, dtype=jnp.float32) / quarter)
    cell_ids = jnp.arange(SEQ, dtype=jnp.int32)
    row_arg = (cell_ids // GRID).astype(jnp.float32)[:, None] * frequencies[None, :]
    col_arg = (cell_ids % GRID).astype(jnp.float32)[:, None] * frequencies[None, :]
    return jnp.concatenate(
        [jnp.sin(col_arg), jnp.cos(col_arg), jnp.sin(row_arg), jnp.cos(row_arg)], axis=1
    )


def time_features(tstep_idx):
    half_freq = FREQ // 2
    frequencies = jnp.exp(-math.log(10000.0) * jnp.arange(half_freq, dtype=jnp.float32) / half_freq)
    angles = (tstep_idx.astype(jnp.float32) + 0.5)[:, None] * frequencies[None, :]
    return jnp.concatenate([jnp.cos(angles), jnp.sin(angles)], axis=1)


def normalize(values):
    centered = values - jnp.mean(values, axis=-1, keepdims=True)
    inv_dev = lax.rsqrt(jnp.mean(centered * centered, axis=-1, keepdims=True) + NORM_EPS)
    return (centered * inv_dev, inv_dev)


def normalize_back(grad_in, normed, inv_dev):
    return inv_dev * (
        grad_in
        - jnp.mean(grad_in, axis=-1, keepdims=True)
        - normed * jnp.mean(grad_in * normed, axis=-1, keepdims=True)
    )


def condition_terms(
    tstep_idx,
    class_ids,
    time_in_weight,
    time_in_bias,
    time_out_weight,
    time_out_bias,
    class_table,
    mod_weight,
    mod_bias,
    final_mod_weight,
    final_mod_bias,
):
    features = time_features(tstep_idx)
    time_hidden = jax.nn.silu(jnp.dot(features, time_in_weight, precision=HIGHEST) + time_in_bias)
    onehot_class = (class_ids[:, None] == jnp.arange(NCLS, dtype=jnp.int32)[None, :]).astype(
        jnp.float32
    )
    condition = (
        jnp.dot(time_hidden, time_out_weight, precision=HIGHEST)
        + time_out_bias
        + jnp.dot(onehot_class, class_table, precision=HIGHEST)
    )
    cond_act = jax.nn.silu(condition)
    modulation = jnp.dot(cond_act, mod_weight, precision=HIGHEST) + mod_bias
    final_mods = jnp.dot(cond_act, final_mod_weight, precision=HIGHEST) + final_mod_bias
    return (modulation, final_mods)


def cosine_total(aligned, dino_f):
    products = jnp.sum(aligned * dino_f, axis=-1)
    return jnp.sum(
        products
        * lax.rsqrt(jnp.sum(aligned * aligned, axis=-1) + NORM_EPS)
        * lax.rsqrt(jnp.sum(dino_f * dino_f, axis=-1) + NORM_EPS)
    )


def matmul(left, right):
    return jnp.dot(left, right, preferred_element_type=jnp.float32)


def row_total(rounded):
    return jnp.sum(rounded.astype(jnp.float32), axis=0)


def body(
    noisy,
    velocity,
    tstep_idx,
    class_ids,
    time_weight,
    dino,
    owner_map,
    adam_flat,
    adam_m,
    adam_v,
    blocks_w,
    stat_left,
    stat_right,
    root_left,
    root_right,
):
    devices = lax.axis_size("dp") * lax.axis_size("shard")
    images = noisy.shape[0]
    seq = noisy.shape[1]
    total_img = images * devices
    rows = images * seq
    fc_ratio = F // D
    flat_low = lax.all_gather(adam_flat.astype(jnp.bfloat16), ("dp", "shard"), axis=0, tiled=True)
    slot_low = lax.all_gather(blocks_w.astype(jnp.bfloat16), "shard", axis=0, tiled=True)
    block_ids = jnp.arange(NBLK, dtype=jnp.int32)
    slot_of = jnp.sum(
        block_ids[:, None] * (owner_map[:, None] == block_ids[None, :]).astype(jnp.int32), axis=0
    )
    blocks = jnp.take(slot_low, slot_of, axis=0)
    w_qkv = jnp.concatenate([blocks[0], blocks[1], blocks[2]], axis=1)
    w_proj = blocks[3]
    w_up = jnp.concatenate([blocks[4 + which] for which in range(fc_ratio)], axis=1)
    w_down = blocks[4 + fc_ratio :].reshape(F, D)
    pieces_low = unflatten(flat_low)
    pieces = [piece.astype(jnp.float32) for piece in pieces_low]
    (
        patch_weight,
        patch_bias,
        time_in_weight,
        time_in_bias,
        time_out_weight,
        time_out_bias,
        class_table,
        mod_weight,
        mod_bias,
        query_bias,
        value_bias,
        proj_bias,
        hidden_bias,
        down_bias,
        final_mod_weight,
        final_mod_bias,
        final_weight,
        final_bias,
        align_weight,
        align_bias,
    ) = pieces
    patch_low = pieces_low[0]
    final_low = pieces_low[16]
    align_low = pieces_low[18]
    cond_weights = (
        time_in_weight,
        time_in_bias,
        time_out_weight,
        time_out_bias,
        class_table,
        mod_weight,
        mod_bias,
        final_mod_weight,
        final_mod_bias,
    )
    (modulation, final_mods), cond_back = jax.vjp(
        functools.partial(condition_terms, tstep_idx, class_ids), *cond_weights
    )
    shift_one, scale_one, gate_one, shift_two, scale_two, gate_two = [
        modulation[:, None, which * D : (which + 1) * D] for which in range(6)
    ]
    final_shift = final_mods[:, None, :D]
    final_scale = final_mods[:, None, D:]
    noisy_low = noisy.astype(jnp.bfloat16).reshape(rows, PD)
    hidden0 = (matmul(noisy_low, patch_low) + patch_bias).reshape(images, seq, D) + position_table()
    norm_one, inv_one = normalize(hidden0)
    act_one = (norm_one * (1.0 + scale_one) + shift_one).astype(jnp.bfloat16).reshape(rows, D)
    qkv_bias = jnp.concatenate([query_bias, jnp.zeros((D,), jnp.float32), value_bias])
    projected = (
        (matmul(act_one, w_qkv) + qkv_bias)
        .astype(jnp.bfloat16)
        .reshape(images, seq, 3, HEADS, HDIM)
    )
    queries = projected[:, :, 0]
    key_part = projected[:, :, 1]
    values = projected[:, :, 2]
    scale_qk = HDIM ** (-0.5)
    scores = (
        jnp.einsum("gqhe,gkhe->ghqk", queries, key_part, preferred_element_type=jnp.float32)
        * scale_qk
    )
    row_max = jnp.max(scores, axis=-1, keepdims=True)
    log_total = row_max + jnp.log(jnp.sum(jnp.exp(scores - row_max), axis=-1, keepdims=True))
    probs_low = jnp.exp(scores - log_total).astype(jnp.bfloat16)
    attended = (
        jnp.einsum("ghqk,gkhe->gqhe", probs_low, values, preferred_element_type=jnp.float32)
        .reshape(rows, D)
        .astype(jnp.bfloat16)
    )
    branch_one = (matmul(attended, w_proj) + proj_bias).reshape(images, seq, D)
    hidden1 = hidden0 + gate_one * branch_one
    norm_two, inv_two = normalize(hidden1)
    act_two = (norm_two * (1.0 + scale_two) + shift_two).astype(jnp.bfloat16).reshape(rows, D)
    inner_pre = matmul(act_two, w_up) + hidden_bias
    gelu_out, gelu_back = jax.vjp(functools.partial(jax.nn.gelu, approximate=True), inner_pre)
    gelu_low = gelu_out.astype(jnp.bfloat16)
    branch_two = (matmul(gelu_low, w_down) + down_bias).reshape(images, seq, D)
    hidden2 = hidden1 + gate_two * branch_two
    norm_three, inv_three = normalize(hidden2)
    act_three = (
        (norm_three * (1.0 + final_scale) + final_shift).astype(jnp.bfloat16).reshape(rows, D)
    )
    output = (matmul(act_three, final_low) + final_bias).reshape(images, seq, PD)
    errors = output - velocity
    main_term = jnp.sum(time_weight[:, None, None] * errors * errors) / (total_img * SEQ * PD)
    hidden1_low = hidden1.astype(jnp.bfloat16).reshape(rows, D)
    aligned = matmul(hidden1_low, align_low) + align_bias
    dino_f = dino.astype(jnp.float32).reshape(rows, DINO)
    cosine_sum, cosine_back = jax.vjp(functools.partial(cosine_total, dino_f=dino_f), aligned)
    align_scale = REPA_WEIGHT / (total_img * SEQ)
    loss_local = main_term - align_scale * cosine_sum
    back_output = (
        (2.0 * time_weight[:, None, None] * errors / (total_img * SEQ * PD))
        .reshape(rows, PD)
        .astype(jnp.bfloat16)
    )
    grad_final = matmul(act_three.T, back_output)
    grad_final_bias = row_total(back_output)
    back_three = matmul(back_output, final_low.T).reshape(images, seq, D)
    grad_final_shift = jnp.sum(back_three, axis=1)
    grad_final_scale = jnp.sum(back_three * norm_three, axis=1)
    back_hidden2 = normalize_back(back_three * (1.0 + final_scale), norm_three, inv_three)
    back_branch_two = (back_hidden2 * gate_two).reshape(rows, D).astype(jnp.bfloat16)
    grad_gate_two = jnp.sum(back_hidden2 * branch_two, axis=1)
    grad_down = matmul(gelu_low.T, back_branch_two)
    grad_down_bias = row_total(back_branch_two)
    back_inner = gelu_back(matmul(back_branch_two, w_down.T))[0].astype(jnp.bfloat16)
    grad_up = matmul(act_two.T, back_inner)
    grad_hidden_bias = row_total(back_inner)
    back_two = matmul(back_inner, w_up.T).reshape(images, seq, D)
    grad_shift_two = jnp.sum(back_two, axis=1)
    grad_scale_two = jnp.sum(back_two * norm_two, axis=1)
    back_aligned = cosine_back(jnp.asarray(-align_scale, jnp.float32))[0].astype(jnp.bfloat16)
    grad_align = matmul(hidden1_low.T, back_aligned)
    grad_align_bias = row_total(back_aligned)
    back_hidden1 = (
        back_hidden2
        + normalize_back(back_two * (1.0 + scale_two), norm_two, inv_two)
        + matmul(back_aligned, align_low.T).reshape(images, seq, D)
    )
    back_branch_one = (back_hidden1 * gate_one).reshape(rows, D).astype(jnp.bfloat16)
    grad_gate_one = jnp.sum(back_hidden1 * branch_one, axis=1)
    grad_proj = matmul(attended.T, back_branch_one)
    grad_proj_bias = row_total(back_branch_one)
    back_attended = (
        matmul(back_branch_one, w_proj.T).astype(jnp.bfloat16).reshape(images, seq, HEADS, HDIM)
    )
    back_probs = jnp.einsum(
        "gqhe,gkhe->ghqk", back_attended, values, preferred_element_type=jnp.float32
    )
    grad_values = jnp.einsum(
        "ghqk,gqhe->gkhe", probs_low, back_attended, preferred_element_type=jnp.float32
    )
    scores_again = (
        jnp.einsum("gqhe,gkhe->ghqk", queries, key_part, preferred_element_type=jnp.float32)
        * scale_qk
    )
    probs_again = jnp.exp(scores_again - log_total)
    back_scores = (
        probs_again * (back_probs - jnp.sum(back_probs * probs_again, axis=-1, keepdims=True))
    ).astype(jnp.bfloat16)
    grad_queries = (
        jnp.einsum("ghqk,gkhe->gqhe", back_scores, key_part, preferred_element_type=jnp.float32)
        * scale_qk
    )
    grad_keys = (
        jnp.einsum("ghqk,gqhe->gkhe", back_scores, queries, preferred_element_type=jnp.float32)
        * scale_qk
    )
    back_projected = (
        jnp.stack([grad_queries, grad_keys, grad_values], axis=2)
        .reshape(rows, 3 * D)
        .astype(jnp.bfloat16)
    )
    grad_qkv = matmul(act_one.T, back_projected)
    grad_qkv_bias = row_total(back_projected)
    back_one = matmul(back_projected, w_qkv.T).reshape(images, seq, D)
    grad_shift_one = jnp.sum(back_one, axis=1)
    grad_scale_one = jnp.sum(back_one * norm_one, axis=1)
    back_hidden0 = (
        (back_hidden1 + normalize_back(back_one * (1.0 + scale_one), norm_one, inv_one))
        .reshape(rows, D)
        .astype(jnp.bfloat16)
    )
    grad_patch = matmul(noisy_low.T, back_hidden0)
    grad_patch_bias = row_total(back_hidden0)
    grad_modulation = jnp.concatenate(
        [
            grad_shift_one,
            grad_scale_one,
            grad_gate_one,
            grad_shift_two,
            grad_scale_two,
            grad_gate_two,
        ],
        axis=1,
    )
    grad_final_mods = jnp.concatenate([grad_final_shift, grad_final_scale], axis=1)
    cond_grads = cond_back((grad_modulation, grad_final_mods))
    grad_list = (
        [grad_patch, grad_patch_bias]
        + list(cond_grads[:7])
        + [
            grad_qkv_bias[:D],
            grad_qkv_bias[2 * D :],
            grad_proj_bias,
            grad_hidden_bias,
            grad_down_bias,
            cond_grads[7],
            cond_grads[8],
            grad_final,
            grad_final_bias,
            grad_align,
            grad_align_bias,
        ]
    )
    flat_grad = jnp.concatenate(
        [gradient_part.reshape(-1) for gradient_part in grad_list]
        + [jnp.zeros((ADAM_PAD - ADAM_LEN,), jnp.float32)]
    )
    grad_model = jnp.concatenate(
        [
            grad_qkv.reshape(D, 3, D).transpose(1, 0, 2),
            grad_proj[None],
            grad_up.reshape(D, fc_ratio, D).transpose(1, 0, 2),
            grad_down.reshape(fc_ratio, D, D),
        ],
        axis=0,
    )
    grad_slot = jnp.take(grad_model, owner_map, axis=0)
    flat_owned = lax.psum_scatter(flat_grad, ("dp", "shard"), scatter_dimension=0, tiled=True)
    loss_total = lax.psum(loss_local, ("dp", "shard"))
    summed = lax.psum(grad_slot, "dp")
    owned = lax.psum_scatter(
        summed.astype(jnp.bfloat16), "shard", scatter_dimension=0, tiled=True
    ).astype(jnp.float32)
    new_left = STAT_BETA * stat_left + (1.0 - STAT_BETA) * jnp.einsum(
        "bij,bkj->bik", owned, owned, precision=HIGHEST
    )
    new_right = STAT_BETA * stat_right + (1.0 - STAT_BETA) * jnp.einsum(
        "bji,bjk->bik", owned, owned, precision=HIGHEST
    )
    left_applied = jnp.einsum("bij,bjk->bik", root_left, owned, precision=HIGHEST)
    direction = jnp.einsum("bij,bjk->bik", left_applied, root_right, precision=HIGHEST)
    root_mean = jnp.sqrt(jnp.mean(direction * direction, axis=(1, 2), keepdims=True))
    block_update = -SHAMPOO_RATE * (direction / (root_mean + RMS_EPS) + DECAY_RATE * blocks_w)
    new_m = BETA_ONE * adam_m + (1.0 - BETA_ONE) * flat_owned
    new_v = BETA_TWO * adam_v + (1.0 - BETA_TWO) * flat_owned * flat_owned
    corrected_m = new_m / (1.0 - BETA_ONE**STEP)
    corrected_v = new_v / (1.0 - BETA_TWO**STEP)
    adam_update = -ADAM_RATE * (
        corrected_m / (jnp.sqrt(corrected_v) + ADAM_EPS) + DECAY_RATE * adam_flat
    )
    return (loss_total, block_update, new_left, new_right, adam_update, new_m, new_v)


def solution(mesh):
    return jax.shard_map(
        body,
        mesh=mesh,
        in_specs=(
            P(("dp", "shard"), None, None),
            P(("dp", "shard"), None, None),
            P(("dp", "shard")),
            P(("dp", "shard")),
            P(("dp", "shard")),
            P(("dp", "shard"), None, None),
            P(),
            P(("dp", "shard")),
            P(("dp", "shard")),
            P(("dp", "shard")),
            P("shard", None, None),
            P("shard", None, None),
            P("shard", None, None),
            P("shard", None, None),
            P("shard", None, None),
        ),
        out_specs=(
            P(),
            P("shard", None, None),
            P("shard", None, None),
            P("shard", None, None),
            P(("dp", "shard")),
            P(("dp", "shard")),
            P(("dp", "shard")),
        ),
        check_vma=False,
    )
```

profile of v0, /device:TPU:0, one launch (start us, length us, event | category | flops | bytes accessed | tf_op | source)
XLA Modules:
  0.0 797.5 jit_solution(3456417252762726016)
XLA Ops:
  7.3 2.6 convert_element_type.209
  17.3 26.3 %all-gather.5.cloned.1.call-done = bf16[12,384,384]{2,1,0:T(8,128)(2,1)} async-done(((bf16[3,384,384]{2,1,0:T(8,128)(2,1)}), bf16[12,384,384]{2,1,0:T(8,128)(2,1)}) %all-gather.5.cloned.1.call-update) | async-done | bytes 3538960 | tf_op jit(solution)/shard_map/all_gather | solution.py:172
  43.6 5.1 gather_fusion
  48.7 2.5 broadcast_select_fusion.1
  54.7 54.4 %all-gather.3.cloned.1.call-done = bf16[2129920]{0:T(1024)(128)(2,1)} async-done(((bf16[66560]{0:T(1024)(128)(2,1)}), bf16[2129920]{0:T(1024)(128)(2,1)}) %all-gather.3.cloned.1.call-update) | async-done | bytes 4259856 | tf_op jit(solution)/shard_map/all_gather | solution.py:171
  109.1 1.7 fusion.108
  121.1 1.9 slice.198
  122.9 3.3 reshape.435
  137.7 2.9 fusion.19
  140.5 4.3 copy.90
  144.9 6.1 reshape.436
  151.0 2.4 fusion.110
  159.4 3.6 fusion.106
  162.9 1.8 multiply_reduce_fusion.12
  165.3 1.9 fusion.26
  168.0 1.8 convolution_add_fusion.1
  169.8 3.8 fusion.104
  174.2 1.8 multiply_reduce_fusion.11
  178.0 1.9 fusion.27
  182.8 2.9 multiply_reduce_fusion.7
  185.8 2.2 convert_reduce_fusion.3
  188.0 7.3 fusion.13
  195.3 5.1 convert_reduce_fusion
  200.5 3.1 fusion.33
  203.7 3.5 multiply_reduce_fusion.2
  210.2 3.0 convert_reduce_fusion.4
  214.0 2.5 convolution_convert_fusion.1
  216.6 2.3 copy.98
  218.8 2.8 reshape.446
  221.7 7.7 multiply_reduce_fusion
  229.4 6.3 multiply_convert_fusion
  237.3 2.0 multiply_bitcast_fusion
  239.2 2.2 convolution_bitcast_fusion.2
  241.5 2.2 multiply_reduce_fusion.4
  247.1 2.5 multiply_reduce_fusion.6
  249.7 2.7 convert_reduce_fusion.5
  252.4 4.8 fusion.95
  257.8 2.1 fusion.113
  259.9 2.3 fusion.55
  262.2 1.7 fusion.91
  265.5 3.4 fusion.46
  268.9 2.2 fusion.68
  271.7 3.4 copy.104
  276.5 4.7 reshape.451
  283.6 2.1 fusion.72
  285.7 1.8 reshape.448
  287.5 2.0 convolution_bitcast_fusion.4
  291.9 2.4 reshape.452
  300.5 87.2 %concatenate.35 = f32[2129920]{0:T(1024)} concatenate(f32[6144]{0:T(1024)} %reshape.447, f32[384]{0:T(512)} %get-tuple-element.39, f32[98304]{0:T(1024)S(1)} %copy-done.57, f32[384]{0:T(512)} %get-tuple-element.37, f32[147456]{0:T(1024)S(1)} %reshape.449, f32[384]{0:T(512)} %get-tuple-element.110, f32[384384]{0:T(1024)} %reshape.450, f32[884736]{0:T(1024)} %reshape.451, ...), dimensions={0} | concatenate | bytes 17039360 | tf_op jit(solution)/shard_map/concatenate | solution.py:381
  387.8 2.3 copy.141
  391.3 4.9 copy.131
  396.2 5.1 convolution_bitcast_fusion
  401.3 4.7 copy.132
  406.1 4.2 fusion.114
  410.3 3.3 pad_maximum_fusion
  413.5 7.0 gather_fusion.1
  420.6 6.6 broadcast_select_fusion
  427.1 306.0 %all-reduce.5 = bf16[12,384,384]{2,1,0:T(8,128)(2,1)} all-reduce(f32[12,384,384]{2,1,0:T(8,128)} %broadcast_select_fusion), channel_id=1, replica_groups=mesh['dp'=8,'shard'=4] {'dp'}, use_global_device_ids=true, to_apply=%region_20.21 | all-reduce | flops 1769472 | bytes 10616832 | tf_op jit(solution)/shard_map/psum | solution.py:397
  734.7 40.7 %psum.14 = f32[]{:T(128)} all-reduce(f32[]{:T(128)S(6)} %sub.143), channel_id=1, replica_groups=mesh['dp'=8,'shard'=4] {'dp','shard'}, use_global_device_ids=true, to_apply=%region_14.15 | all-reduce | flops 1 | bytes 8 | tf_op jit(solution)/shard_map/psum | solution.py:396
  775.4 2.2 add_multiply_fusion.1
  777.5 3.0 fusion.115
  780.6 3.8 multiply_reduce_fusion.3
  786.8 2.0 multiply_add_fusion
  788.8 2.0 multiply_add_fusion.1
  (328 shorter events, 73.1 us)
Async XLA Ops:
  7.2 773.4 %copy-start = (f32[3,384,384]{2,1,0:T(8,128)S(1)}, f32[3,384,384]{2,1,0:T(8,128)}, u32[]{:S(2)}) copy-start(f32[3,384,384]{2,1,0:T(8,128)} %param.29) | copy-start | bytes 5308420
  7.2 4.5 copy-start.78
  7.2 5.1 copy-start.22
  7.2 36.4 %all-gather.5.cloned.1.call-start = ((), (), s32[]{:S(2)}) async-start(), calls=%async_computation.2 | async-start | bytes 4423680 | tf_op jit(solution)/shard_map/all_gather | solution.py:172
  9.9 3.5 copy-start.97
  9.9 99.2 %all-gather.3.cloned.1.call-start = ((), (), s32[]{:S(2)}) async-start(), calls=%async_computation.1 | async-start | bytes 4392960 | tf_op jit(solution)/shard_map/all_gather | solution.py:171
  11.6 5.1 copy-start.98
  11.6 5.1 copy-start.96
  11.6 763.7 %all-reduce.4.cloned.1.call-start = ((), (), s32[]{:S(2)}) async-start(), calls=%async_computation.4 | async-start | bytes 17039360
  17.3 114.4 %copy-start.88 = (f32[4,128]{1,0:T(4,128)}, f32[4,128]{1,0:T(4,128)S(1)}, u32[]{:S(2)}) copy-start(f32[4,128]{1,0:T(4,128)S(1)} %get-tuple-element.90) | copy-start | bytes 6148
  17.3 114.4 %copy-start.90 = (f32[4,128]{1,0:T(4,128)}, f32[4,128]{1,0:T(4,128)S(1)}, u32[]{:S(2)}) copy-start(f32[4,128]{1,0:T(4,128)S(1)} %get-tuple-element.91) | copy-start | bytes 6148
  128.4 3.3 copy-start.67
  128.4 3.5 copy-start.49
  128.4 3.8 copy-start.48
  128.4 3.8 copy-start.93
  130.0 3.8 copy-start.41
  130.1 4.8 copy-start.17
  131.7 4.6 copy-start.86
  131.9 4.4 copy-start.8
  136.3 4.3 copy-start.80
  159.1 3.8 copy-start.30
  169.8 3.8 copy-start.13
  169.8 6.8 copy-start.82
  178.0 3.2 copy-start.79
  178.0 4.8 copy-start.5
  178.0 4.8 copy-start.10
  178.0 4.8 copy-start.84
  178.0 4.8 copy-start.91
  180.8 7.1 slice-start.2
  182.8 2.9 copy-start.71
  182.8 5.2 slice-start.3
  188.0 7.3 copy-start.66
  195.3 5.1 copy-start.3
  195.3 5.1 copy-start.59
  195.3 5.1 copy-start.61
  195.3 5.1 copy-start.63
  195.3 5.1 copy-start.65
  200.5 3.2 copy-start.85
  203.7 3.5 copy-start.6
  203.7 3.5 copy-start.11
  203.7 3.5 copy-start.24
  203.7 3.5 copy-start.83
  210.0 3.1 copy-start.20
  221.7 17.5 %slice-start = ((s8[6291456]{0:T(1024)(128)(4,1)}), s8[4194304]{0:T(1024)(128)(4,1)S(1)}, s32[]{:S(2)}) async-start(s8[6291456]{0:T(1024)(128)(4,1)} %bitcast.283), calls=%async_computation.5 | async-start | bytes 8388608
  229.4 6.4 copy-start.26
  229.4 9.8 %slice-start.1 = ((s8[6291456]{0:T(1024)(128)(4,1)}), s8[2097152]{0:T(1024)(128)(4,1)S(1)}, s32[]{:S(2)}) async-start(s8[6291456]{0:T(1024)(128)(4,1)} %bitcast.283), calls=%async_computation.6 | async-start | bytes 4194304
  252.4 4.8 copy-start.42
  252.4 5.3 copy-start.18
  257.2 2.7 copy-start.94
  257.7 6.1 copy-start.50
  257.7 7.7 copy-start.4
  265.5 6.2 copy-start.16
  271.6 3.4 copy-start.28
  271.6 3.4 copy-start.31
  276.5 4.7 copy-start.40
  282.4 8.4 %copy-start.38 = (f32[384,768]{1,0:T(8,128)S(1)}, f32[384,768]{1,0:T(8,128)}, u32[]{:S(2)}) copy-start(f32[384,768]{1,0:T(8,128)} %fusion.46) | copy-start | bytes 3538948
  291.9 6.4 copy-start.33
  291.9 8.6 %copy-start.57 = (f32[98304]{0:T(1024)S(1)}, f32[98304]{0:T(1024)}, u32[]{:S(2)}) copy-start(f32[98304]{0:T(1024)} %reshape.448) | copy-start | bytes 1179652
  387.7 389.8 %reduce-scatter.2.cloned.1.call-start = ((), (), s32[]{:S(2)}) async-start(), calls=%async_computation.3 | async-start | bytes 4423680 | tf_op jit(solution)/shard_map/reduce_scatter | solution.py:398
  406.1 4.2 copy-start.52
  406.1 4.2 copy-start.53
  413.5 7.0 copy-start.95
  733.2 44.4 %copy-start.54 = (f32[3,384,384]{2,1,0:T(8,128)S(1)}, f32[3,384,384]{2,1,0:T(8,128)}, u32[]{:S(2)}) copy-start(f32[3,384,384]{2,1,0:T(8,128)} %param.28) | copy-start | bytes 5308420
  780.6 3.8 copy-start.29
  (43 other events, 81.9 us)
Sparse Core Ops, SparseCore 0:
  10.1 33.4 all-gather.4
  47.1 61.9 all-gather.2
  387.8 243.0 all-reduce.3
  733.3 39.5 reduce-scatter.1
where the time goes:
time: 810 us; the launch traced here: 798 us
  blocking collectives  347 us (43%)
  local copies, waits for them, and re-layouts  186 us (23%)
  matrix products  103 us (13%)
  waiting for transfers between devices  80.8 us (10%)
  other arithmetic  64.9 us (8%)
  between operations  16.6 us (2%)
    psum x1, blocking collectives, body(): summed = lax.psum(grad_slot, 'dp')  306 us
    concatenate x1, local copies, waits for them, and re-layouts, body(): jnp.concatenate([gradient_part.reshape(-1) for gradient_part in grad_list...  87.2 us
    dot_general x20, matrix products, matmul(): return jnp.dot(left, right, preferred_element_type=jnp.float32)  57.1 us
    all_gather x1, waiting for transfers between devices, body(): lax.all_gather(adam_flat.astype(jnp.bfloat16), ('dp', 'shard'), axis=0, t...  54.4 us
    psum x1, blocking collectives, body(): loss_total = lax.psum(loss_local, ('dp', 'shard'))  40.7 us
    all_gather x1, waiting for transfers between devices, body(): lax.all_gather(blocks_w.astype(jnp.bfloat16), 'shard', axis=0, tiled=True)  26.3 us
  transfers between devices with their start and end apart: 4, of which 2 were waited for; matrix products, arithmetic and copies ran while one was open for 7% of the time, Pallas kernels for 0%

commit v1 on v0

--- a/solution.py
+++ b/solution.py
@@ -32,6 +32,18 @@
 NORM_EPS = 1e-06
 
 
+def gather_by_bits(x, axis, dim):
+    ways, here = (lax.axis_size(axis), lax.axis_index(axis))
+    grown, reach = (x, 1)
+    while reach < ways:
+        theirs = lax.ppermute(grown, axis, [(d, d ^ reach) for d in range(ways)])
+        mine_first = jnp.concatenate([grown, theirs], axis=dim)
+        theirs_first = jnp.concatenate([theirs, grown], axis=dim)
+        grown = jnp.where(here & reach == 0, mine_first, theirs_first)
+        reach = 2 * reach
+    return grown
+
+
 def segment_shapes():
     return [
         (PD, D),
@@ -168,7 +180,7 @@
     total_img = images * devices
     rows = images * seq
     fc_ratio = F // D
-    flat_low = lax.all_gather(adam_flat.astype(jnp.bfloat16), ("dp", "shard"), axis=0, tiled=True)
+    flat_low = gather_by_bits(adam_flat.astype(jnp.bfloat16), ("dp", "shard"), 0)
     slot_low = lax.all_gather(blocks_w.astype(jnp.bfloat16), "shard", axis=0, tiled=True)
     block_ids = jnp.arange(NBLK, dtype=jnp.int32)
     slot_of = jnp.sum(

time: 810 us -> 939 us (1.16)
  local copies, waits for them, and re-layouts: 186 us -> 269 us
  other arithmetic: 64.9 us -> 91.6 us
  waiting for transfers between devices: 80.8 us -> 92.9 us
    ppermute x0 -> x5, waiting for transfers between devices: none -> 92.8 us  [gather_by_bits(): theirs = lax.ppermute(grown, axis, [(d, d ^ reach) for d in range(ways)])]
    concatenate x0 -> x10, local copies, waits for them, and re-layouts: none -> 62.5 us  [gather_by_bits(): mine_first = jnp.concatenate([grown, theirs], axis=dim)]
    all_gather x1 -> x0, waiting for transfers between devices: 54.4 us -> none  [body(): lax.all_gather(adam_flat.astype(jnp.bfloat16), ('dp', 'shard'), axis=0, t...]
    select_n x0 -> x9, other arithmetic: none -> 28.8 us  [gather_by_bits(): grown = jnp.where(here & reach == 0, mine_first, theirs_first)]
    all_gather x1, waiting for transfers between devices: 26.3 us -> 0.01 us  [body(): lax.all_gather(blocks_w.astype(jnp.bfloat16), 'shard', axis=0, tiled=True)]
    reshape x0 -> x3, local copies, waits for them, and re-layouts: none -> 9.75 us  [the longest x1 3.59 us: body(): (matmul(noisy_low, patch_low) + patch_bias).reshape(images, seq, D)]
  transfers between devices with their start and end apart: 4 -> 8, of which waited for: 2 -> 4; matrix products, arithmetic and copies ran while one was open for 7% -> 19% of each run, Pallas kernels for 0% -> 0%
where the time goes in v1:
time: 939 us; the launch traced here: 929 us
  blocking collectives  348 us (37%)
  local copies, waits for them, and re-layouts  269 us (29%)
  matrix products  103 us (11%)
  waiting for transfers between devices  92.9 us (10%)
  other arithmetic  91.6 us (10%)
  between operations  16.8 us (2%)
    psum x1, blocking collectives, body(): summed = lax.psum(grad_slot, 'dp')  309 us
    ppermute x5, waiting for transfers between devices, gather_by_bits(): theirs = lax.ppermute(grown, axis, [(d, d ^ reach) for d in range(ways)])  92.8 us
    concatenate x1, local copies, waits for them, and re-layouts, body(): jnp.concatenate([gradient_part.reshape(-1) for gradient_part in grad_list...  78.1 us
    concatenate x10, local copies, waits for them, and re-layouts, gather_by_bits(): mine_first = jnp.concatenate([grown, theirs], axis=dim)  62.5 us
    dot_general x20, matrix products, matmul(): return jnp.dot(left, right, preferred_element_type=jnp.float32)  54.4 us
    psum x1, blocking collectives, body(): loss_total = lax.psum(loss_local, ('dp', 'shard'))  39.6 us
    select_n x9, other arithmetic, gather_by_bits(): grown = jnp.where(here & reach == 0, mine_first, theirs_first)  28.8 us
  transfers between devices with their start and end apart: 8, of which 4 were waited for; matrix products, arithmetic and copies ran while one was open for 19% of the time, Pallas kernels for 0%

profile of v1, /device:TPU:0, one launch (start us, length us, event | category | flops | bytes accessed | tf_op | source)
XLA Modules:
  0.0 929.3 jit_solution(3737484209795014844)
XLA Ops:
  8.9 2.5 convert_element_type.209
  18.6 2.7 collective-permute-start.1
  22.5 3.2 copy.214
  27.0 2.5 concatenate.106
  41.1 6.4 collective-permute-done.2
  47.5 2.5 maximum_select_fusion.4
  51.2 4.0 concatenate.110
  55.2 3.8 copy.174
  61.5 12.6 %collective-permute-done.3 = bf16[532480]{0:T(1024)(128)(2,1)S(1)} collective-permute-done((bf16[532480]{0:T(1024)(128)(2,1)}, bf16[532480]{0:T(1024)(128)(2,1)S(1)}, u32[]{:S(2)}, u32[]{:S(2)}) %collective-permute-start.3) | collective-permute-done | bytes 1064992 | tf_op jit(solution)/shard_map/ppermute | solution.py:39
  74.0 9.6 %maximum_select_fusion.2 = bf16[1064960]{0:T(1024)(128)(2,1)} fusion(bf16[532480]{0:T(1024)(128)(2,1)S(1)} %collective-permute-done.3, bf16[532480]{0:T(1024)(128)(2,1)} %maximum_select_fusion.4, pred[]{:T(512)S(6)} %eq.44), kind=kLoop, calls=%fused_computation.56 | loop fusion | flops 9584640 | bytes 4259841 | tf_op jit(solution)/shard_map/jit(_where)/select_n | solution.py:42
  86.1 7.4 concatenate.113
  93.5 7.1 copy.176
  100.6 3.4 maximum_select_fusion.1
  104.0 72.3 %collective-permute-done.4 = bf16[1064960]{0:T(1024)(128)(2,1)} collective-permute-done((bf16[1064960]{0:T(1024)(128)(2,1)}, bf16[1064960]{0:T(1024)(128)(2,1)}, u32[]{:S(2)}, u32[]{:S(2)}) %collective-permute-start.4) | collective-permute-done | bytes 2129952 | tf_op jit(solution)/shard_map/ppermute | solution.py:39
  176.3 6.8 maximum_select_fusion
  190.1 17.6 %concatenate.116 = bf16[66560,16]{1,0:T(8,128)(2,1)} reshape(bf16[1064960]{0:T(1024)(128)(2,1)} %collective-permute-done.4) | data formatting | bytes 4259840 | tf_op jit(solution)/shard_map/concatenate | solution.py:40
  207.7 13.4 %copy.178 = bf16[66560,16]{0,1:T(8,128)(2,1)} copy(bf16[66560,16]{1,0:T(8,128)(2,1)} %concatenate.116) | data formatting | bytes 4259840 | tf_op jit(solution)/shard_map/concatenate | solution.py:40
  225.3 3.6 reshape.444
  254.9 3.0 fusion.100
  257.9 3.6 copy.220
  266.7 5.1 gather_fusion
  271.9 2.5 broadcast_select_fusion.1
  278.2 3.0 fusion.19
  281.1 4.3 copy.157
  285.4 5.7 reshape.445
  300.8 2.9 fusion.99
  305.1 2.5 add_convert_fusion.2
  309.7 4.3 fusion.98
  316.9 3.0 copy.223
  319.9 3.1 copy.224
  323.1 3.1 add_convert_fusion.1
  331.7 7.2 fusion.13
  338.9 5.1 convert_reduce_fusion
  344.1 3.1 fusion.25
  347.1 3.0 copy.184
  350.2 2.4 multiply_reduce_fusion.16
  352.7 3.1 multiply_reduce_fusion.2
  359.2 3.2 convert_reduce_fusion.4
  363.9 2.5 convolution_convert_fusion.1
  368.7 2.6 reshape.455
  371.3 4.4 convolution_bitcast_fusion.2
  375.8 7.2 multiply_reduce_fusion
  383.0 4.5 multiply_convert_fusion
  389.6 3.4 copy.191
  396.7 2.5 multiply_reduce_fusion.6
  399.3 2.5 convert_reduce_fusion.5
  409.4 4.7 fusion.89
  417.6 3.2 fusion.38
  420.8 4.8 copy.222
  425.5 4.7 copy.221
  430.3 4.8 convolution_bitcast_fusion
  436.2 2.4 convolution_bitcast_fusion.1
  445.3 4.6 reshape.460
  451.2 2.6 reshape.461
  454.4 2.4 reshape.463
  456.9 78.1 %concatenate.122 = f32[2129920]{0:T(1024)} concatenate(f32[6144]{0:T(1024)S(1)} %reshape.456, f32[384]{0:T(512)S(1)} %copy-done.114, f32[98304]{0:T(1024)} %reshape.457, f32[384]{0:T(512)S(1)} %copy-done.116, f32[147456]{0:T(1024)} %reshape.458, f32[384]{0:T(512)S(1)} %copy-done.115, f32[384384]{0:T(1024)S(1)} %copy-done.45, f32[884736]{0:T(1024)} %reshape.460, ...), dimensions={0} | concatenate | bytes 17039360 | tf_op jit(solution)/shard_map/concatenate | solution.py:393
  536.1 3.8 fusion.105
  540.0 3.3 pad_maximum_fusion
  543.3 7.5 gather_fusion.1
  550.8 6.7 broadcast_select_fusion
  557.4 308.7 %all-reduce.5 = bf16[12,384,384]{2,1,0:T(8,128)(2,1)} all-reduce(f32[12,384,384]{2,1,0:T(8,128)} %broadcast_select_fusion), channel_id=1, replica_groups=mesh['dp'=8,'shard'=4] {'dp'}, use_global_device_ids=true, to_apply=%region_20.21 | all-reduce | flops 1769472 | bytes 10616832 | tf_op jit(solution)/shard_map/psum | solution.py:409
  867.5 39.6 %psum.14 = f32[]{:T(128)} all-reduce(f32[]{:T(128)S(6)} %sub.143), channel_id=1, replica_groups=mesh['dp'=8,'shard'=4] {'dp','shard'}, use_global_device_ids=true, to_apply=%region_14.15 | all-reduce | flops 1 | bytes 8 | tf_op jit(solution)/shard_map/psum | solution.py:408
  909.3 3.0 fusion.106
  912.3 3.8 multiply_reduce_fusion.3
  (440 shorter events, 139.3 us)
Async XLA Ops:
  7.2 905.1 %copy-start = (f32[3,384,384]{2,1,0:T(8,128)S(1)}, f32[3,384,384]{2,1,0:T(8,128)}, u32[]{:S(2)}) copy-start(f32[3,384,384]{2,1,0:T(8,128)} %param.29) | copy-start | bytes 5308420
  7.2 259.6 %all-gather.2.cloned.1.call-start = ((), (), s32[]{:S(2)}) async-start(), calls=%async_computation.1 | async-start | bytes 4423680 | tf_op jit(solution)/shard_map/all_gather | solution.py:184
  8.3 3.2 copy-start.128
  8.3 5.1 copy-start.81
  8.3 6.3 copy-start.125
  8.4 6.8 copy-start.11
  8.4 9.0 collective-permute-start
  11.4 895.7 %all-reduce.4.cloned.1.call-start = ((), (), s32[]{:S(2)}) async-start(), calls=%async_computation.3 | async-start | bytes 17039360
  17.4 8.3 copy-start.37
  18.6 14.6 %collective-permute-start.1 = (bf16[133120]{0:T(1024)(128)(2,1)S(1)}, bf16[133120]{0:T(1024)(128)(2,1)S(1)}, u32[]{:S(2)}, u32[]{:S(2)}) collective-permute-start(bf16[133120]{0:T(1024)(128)(2,1)S(1)} %maximum_select_fusion.7), channel_id=1, source_target_pairs={{0,2},{1,3},{2,0},{3,1},{4,6},{5,7},{6,4},{7,5},{8,10},{9,11},{10,... | collective-permute-start | bytes 798728 | tf_op jit(solution)/shard_map/ppermute | solution.py:39
  22.5 3.2 copy-start.84
  27.0 205.3 %copy-start.99 = (f32[4,128]{1,0:T(4,128)}, f32[4,128]{1,0:T(4,128)S(1)}, u32[]{:S(2)}) copy-start(f32[4,128]{1,0:T(4,128)S(1)} %get-tuple-element.90) | copy-start | bytes 6148
  27.0 205.3 %copy-start.101 = (f32[4,128]{1,0:T(4,128)}, f32[4,128]{1,0:T(4,128)S(1)}, u32[]{:S(2)}) copy-start(f32[4,128]{1,0:T(4,128)S(1)} %get-tuple-element.91) | copy-start | bytes 6148
  34.1 13.4 %collective-permute-start.2 = (bf16[266240]{0:T(1024)(128)(2,1)}, bf16[266240]{0:T(1024)(128)(2,1)S(1)}, u32[]{:S(2)}, u32[]{:S(2)}) collective-permute-start(bf16[266240]{0:T(1024)(128)(2,1)} %maximum_select_fusion.6), channel_id=1, source_target_pairs={{0,4},{1,5},{2,6},{3,7},{4,0},{5,1},{6,2},{7,3},{8,12},{9,13},{10,... | collective-permute-start | bytes 1597448 | tf_op jit(solution)/shard_map/ppermute | solution.py:39
  50.0 24.1 %collective-permute-start.3 = (bf16[532480]{0:T(1024)(128)(2,1)}, bf16[532480]{0:T(1024)(128)(2,1)S(1)}, u32[]{:S(2)}, u32[]{:S(2)}) collective-permute-start(bf16[532480]{0:T(1024)(128)(2,1)} %maximum_select_fusion.4), channel_id=1, source_target_pairs={{0,8},{1,9},{2,10},{3,11},{4,12},{5,13},{6,14},{7,15},{8,0},{9,1},... | collective-permute-start | bytes 3194888 | tf_op jit(solution)/shard_map/ppermute | solution.py:39
  83.7 92.7 %collective-permute-start.4 = (bf16[1064960]{0:T(1024)(128)(2,1)}, bf16[1064960]{0:T(1024)(128)(2,1)}, u32[]{:S(2)}, u32[]{:S(2)}) collective-permute-start(bf16[1064960]{0:T(1024)(128)(2,1)} %maximum_select_fusion.2), channel_id=1, source_target_pairs={{0,16},{1,17},{2,18},{3,19},{4,20},{5,21},{6,22},{7,23},{8,24},{9,... | collective-permute-start | bytes 6389768 | tf_op jit(solution)/shard_map/ppermute | solution.py:39
  183.2 4.2 copy-start.7
  207.7 13.4 %copy-start.51 = (bf16[294912]{0:T(1024)(128)(2,1)S(1)}, bf16[294912]{0:T(1024)(128)(2,1)}, u32[]{:S(2)}) copy-start(bf16[294912]{0:T(1024)(128)(2,1)} %get-tuple-element.53) | copy-start | bytes 1769476
  228.8 9.5 %copy-start.8 = (bf16[384,2304]{1,0:T(8,128)(2,1)}, bf16[384,2304]{1,0:T(8,128)(2,1)S(1)}, u32[]{:S(2)}) copy-start(bf16[384,2304]{1,0:T(8,128)(2,1)S(1)} %reshape.444) | copy-start | bytes 5308420
  257.9 7.4 copy-start.2
  257.9 5.0 copy-start.110
  257.9 5.0 copy-start.111
  266.7 5.1 copy-start.124
  294.7 2.7 copy-start.1
  299.4 4.3 copy-start.27
  309.6 4.4 copy-start.36
  323.1 3.1 copy-start.13
  323.1 3.3 copy-start.15
  323.1 3.4 copy-start.38
  327.0 17.0 %copy-start.4 = (f32[4,256,384]{2,1,0:T(8,128)}, f32[4,256,384]{2,1,0:T(8,128)S(1)}, u32[]{:S(2)}) copy-start(f32[4,256,384]{2,1,0:T(8,128)S(1)} %multiply_add_fusion.2) | copy-start | bytes 4718596
  327.0 4.6 slice-start.3
  328.0 3.7 slice-start.4
  331.7 7.2 copy-start.68
  338.9 5.2 copy-start.59
  338.9 5.2 copy-start.61
  338.9 5.2 copy-start.63
  338.9 5.2 copy-start.65
  338.9 5.2 copy-start.93
  338.9 5.2 copy-start.94
  352.7 3.1 copy-start.105
  352.7 3.7 copy-start.12
  356.4 2.9 copy-start.52
  357.8 4.7 copy-start.19
  359.2 3.2 copy-start.28
  371.3 4.4 copy-start.34
  371.3 4.4 copy-start.35
  371.3 11.6 %slice-start = ((s8[6291456]{0:T(1024)(128)(4,1)}), s8[4194304]{0:T(1024)(128)(4,1)S(1)}, s32[]{:S(2)}) async-start(s8[6291456]{0:T(1024)(128)(4,1)} %bitcast.248), calls=%async_computation.4 | async-start | bytes 8388608
  375.8 7.2 slice-start.1
  383.0 4.5 copy-start.32
  401.8 2.7 copy-start.48
  401.8 5.4 copy-start.122
  425.5 4.7 copy-start.74
  430.3 4.9 copy-start.25
  436.2 2.7 copy-start.102
  438.7 5.4 copy-start.44
  449.9 3.9 copy-start.30
  454.1 2.7 copy-start.45
  535.0 374.3 %reduce-scatter.2.cloned.1.call-start = ((), (), s32[]{:S(2)}) async-start(), calls=%async_computation.2 | async-start | bytes 4423680 | tf_op jit(solution)/shard_map/reduce_scatter | solution.py:410
  536.1 3.8 copy-start.49
  536.1 3.9 copy-start.50
  536.1 3.9 copy-start.54
  543.3 7.5 copy-start.123
  866.2 43.1 %copy-start.53 = (f32[3,384,384]{2,1,0:T(8,128)S(1)}, f32[3,384,384]{2,1,0:T(8,128)}, u32[]{:S(2)}) copy-start(f32[3,384,384]{2,1,0:T(8,128)} %param.28) | copy-start | bytes 5308420
  912.3 3.8 copy-start.26
  (78 other events, 148.6 us)
Sparse Core Ops, SparseCore 0:
  11.6 37.1 all-gather.1
  535.2 271.5 all-reduce.3
  866.3 39.6 reduce-scatter.1
